TPU v7x, 32 devices: a whole 2x2x4 slice. The times are simulated.
32 devices in a mesh: img: 4 (over y, core), pix: 8 (over z, x).
Axes of the slice: x: 2, y: 2, z: 4, core: 2. Of those that a mesh axis runs over, the one named last changes fastest.
Arguments:
- pixels: float32 [2, 4, 82944, 261], P(None, 'img', 'pix'), may hold values from -6 to 6
- sides: int32 [2], replicated, may hold values from 160 to 288, as said below
- owner: int32 [256], replicated, may hold values from 0 to 255, each once
- master: float32 [256, 128, 128], P(('img', 'pix')), may hold values from -0.375 to 0.375
- left_stat: float32 [256, 128, 128], P(('img', 'pix'))
- right_stat: float32 [256, 128, 128], P(('img', 'pix'))
- left_root: float32 [256, 128, 128], P(('img', 'pix'))
- right_root: float32 [256, 128, 128], P(('img', 'pix'))
- kv_weight: float32 [2, 261, 1024], replicated, may hold values from -0.375 to 0.375
- latent_array: float32 [512, 1024], replicated, may hold values from -6 to 6
- in_gain: float32 [261], replicated, may hold values from 0.5 to 1.5
- lat_gains: float32 [2, 1024], replicated, may hold values from 0.5 to 1.5
- cotangent: float32 [2, 4, 512, 1024], P(None, 'img', 'pix'), may hold values from -6 to 6
Outputs:
- latents_out: float32 [2, 4, 512, 1024], P(None, 'img', 'pix')
- pixel_grad: float32 [2, 4, 82944, 261], P(None, 'img', 'pix')
- new_left: float32 [256, 128, 128], P(('img', 'pix'))
- new_right: float32 [256, 128, 128], P(('img', 'pix'))
- new_master: float32 [256, 128, 128], P(('img', 'pix'))
- new_copy: bfloat16 [256, 128, 128], P(('img', 'pix'))
- kv_grad: float32 [2, 261, 1024], replicated
- new_kv: float32 [2, 261, 1024], replicated
- latent_grad: float32 [512, 1024], replicated
- new_latent: float32 [512, 1024], replicated
- in_gain_grad: float32 [261], replicated
- new_in_gain: float32 [261], replicated
- lat_gain_grad: float32 [2, 1024], replicated
- new_lat_gains: float32 [2, 1024], replicated
Inputs may be any that keep to these rules, and one draw needn't show every extreme that they name: Every image of micro-batch m is sides[m] pixels a side, one of 160, 224 or 288; some micro-batch has 288 and some has a smaller side. Slot p of an image (row by row) is a real pixel when p < sides[m]^2; the rest of the 82944 slots are padding. A permutation: block b lives in slot owner[b]; the slots run in order over the devices of img+pix, an equal number to each.
All inputs are finite; a program needn't handle non-finite values.
Results may differ from a plain program's by a relative error of at most 0.015.
The roundings to bfloat16 on the way count: a program that leaves them out, or rounds other values in their place, can miss the bound.
Values may be sent and summed in bfloat16 or wider, within the bound.
No kernel may reach another device: no remote copies, remote signals or barrier semaphores. Data moves between devices by JAX's collectives and lax.ppermute only.
A program may use at most 448 MiB of HBM per device.

v0:
```python
import math

import jax
import jax.numpy as jnp
from jax import lax
from jax.sharding import PartitionSpec as P

CIN = 261
DL = 1024
LAT = 512
BLK = 128
NBLK = 256


HIGHEST_PRECISION = lax.Precision.HIGHEST


def standardize(values_in):
    average = jnp.mean(values_in, axis=-1, keepdims=True)
    centred = values_in - average
    variance = jnp.mean(centred * centred, axis=-1, keepdims=True)
    return centred * lax.rsqrt(variance + 1e-05)


def gelu_exact(values_in):
    return jax.nn.gelu(values_in, approximate=False)


def unblock(blocks, full_width, block_size):
    per_side = full_width // block_size
    return (
        blocks.reshape(4, per_side, per_side, block_size, block_size)
        .transpose(0, 1, 3, 2, 4)
        .reshape(4, full_width, full_width)
    )


def to_blocks(matrices, full_width, block_size):
    per_side = full_width // block_size
    return (
        matrices.reshape(4, per_side, block_size, per_side, block_size)
        .transpose(0, 1, 3, 2, 4)
        .reshape(4 * per_side * per_side, block_size, block_size)
    )


def normalized(gradient, reduce_axes):
    return gradient / jnp.sqrt(
        jnp.mean(gradient * gradient, axis=reduce_axes, keepdims=True) + 1e-06
    )


def product(pattern, left_side, right_side):
    return jnp.einsum(pattern, left_side, right_side, preferred_element_type=jnp.float32)


def score_exp(query, keys, valid, inv_root):
    scores = product("ld,pd->lp", query, keys) * inv_root
    return jnp.where(valid[None, :], jnp.exp(scores), 0.0)


def latent_pass(
    numerator, denominator, lat_part, cot_rows, own_start, own_count, lat_gain, w_out, w_up, w_down
):
    attended = numerator / denominator[..., None]
    att_low = attended.astype(jnp.bfloat16)
    resid = lat_part[None] + product("mrd,de->mre", att_low, w_out)
    normed, normed_back = jax.vjp(standardize, resid)
    hn_low = (normed * lat_gain).astype(jnp.bfloat16)
    hidden = product("mrd,de->mre", hn_low, w_up)
    active, active_back = jax.vjp(gelu_exact, hidden)
    act_low = active.astype(jnp.bfloat16)
    latents_out = resid + product("mrd,de->mre", act_low, w_down)
    g_mlp = cot_rows.astype(jnp.bfloat16)
    d_active = product("mre,de->mrd", g_mlp, w_down)
    d_hidden = active_back(d_active)[0].astype(jnp.bfloat16)
    d_normed = product("mre,de->mrd", d_hidden, w_up)
    d_resid = cot_rows + normed_back(d_normed * lat_gain)[0]
    d_branch = d_resid.astype(jnp.bfloat16)
    d_attended = product("mre,de->mrd", d_branch, w_out)
    d_numer = d_attended / denominator[..., None]
    d_denom = -jnp.sum(d_attended * numerator / (denominator * denominator)[..., None], axis=-1)

    def own_rows(array):
        return lax.dynamic_slice_in_dim(array, own_start, own_count, 1)

    row_pairs = (
        own_rows(att_low),
        own_rows(d_branch),
        own_rows(hn_low),
        own_rows(d_hidden),
        own_rows(act_low),
        own_rows(g_mlp),
    )
    gain_mlp = jnp.sum(own_rows(d_normed * normed), axis=(0, 1))
    lat_resid = jnp.sum(own_rows(d_resid), axis=0)
    return (own_rows(latents_out), d_numer, d_denom, (row_pairs, gain_mlp, lat_resid))


def shards(
    pixels,
    sides,
    owner,
    master,
    left_stat,
    right_stat,
    left_root,
    right_root,
    kv_weight,
    latent_array,
    in_gain,
    lat_gains,
    cotangent,
):
    micro = pixels.shape[0]
    rows_dev = pixels.shape[2]
    lat_rows = LAT // lax.axis_size("pix")
    pix_start = lax.axis_index("pix") * rows_dev
    row_start = lax.axis_index("pix") * lat_rows
    inv_root = 1.0 / math.sqrt(DL)
    gathered = lax.all_gather(master.astype(jnp.bfloat16), ("img", "pix"), axis=0, tiled=True)
    square = unblock(jnp.take(gathered, owner, axis=0), DL, BLK)
    w_query, w_out, w_up, w_down = (square[0], square[1], square[2], square[3])
    kv_low = kv_weight.astype(jnp.bfloat16)
    w_key, w_value = (kv_low[0], kv_low[1])
    lat_norm, lat_norm_back = jax.vjp(standardize, latent_array)
    lat_low = (lat_norm * lat_gains[0]).astype(jnp.bfloat16)
    query = jnp.dot(lat_low, w_query, preferred_element_type=jnp.float32).astype(jnp.bfloat16)
    positions = pix_start + jnp.arange(rows_dev, dtype=jnp.int32)
    stored = []
    numer_list = []
    denom_list = []
    for micro_index in range(micro):
        pix_std, pix_back = jax.vjp(standardize, pixels[micro_index, 0])
        pix_low = (pix_std * in_gain).astype(jnp.bfloat16)
        keys = jnp.dot(pix_low, w_key, preferred_element_type=jnp.float32).astype(jnp.bfloat16)
        values = jnp.dot(pix_low, w_value, preferred_element_type=jnp.float32).astype(jnp.bfloat16)
        valid = positions < sides[micro_index] * sides[micro_index]
        weights_exp = score_exp(query, keys, valid, inv_root)
        numer_list.append(product("lp,pd->ld", weights_exp.astype(jnp.bfloat16), values))
        denom_list.append(jnp.sum(weights_exp, axis=1))
        stored.append((pix_std, pix_back, pix_low, keys, values, valid))
    numerator = jnp.stack(numer_list)
    denominator = jnp.stack(denom_list)
    numer_all, denom_all = lax.psum((numerator, denominator), "pix")
    cot_all = lax.all_gather(
        cotangent[:, 0].astype(jnp.bfloat16), "pix", axis=1, tiled=True
    ).astype(jnp.float32)
    latents_out, d_numer, d_denom, latent_grads = latent_pass(
        numer_all,
        denom_all,
        latent_array,
        cot_all,
        row_start,
        lat_rows,
        lat_gains[1],
        w_out,
        w_up,
        w_down,
    )
    row_pairs, gain_mlp, lat_resid = latent_grads
    d_numer_low = d_numer.astype(jnp.bfloat16)
    query_sum = jnp.zeros((LAT, DL), jnp.float32)
    key_grad = jnp.zeros((CIN, DL), jnp.float32)
    value_grad = jnp.zeros((CIN, DL), jnp.float32)
    gain_input = jnp.zeros((CIN,), jnp.float32)
    pixel_list = []
    for micro_index in range(micro):
        pix_std, pix_back, pix_low, keys, values, valid = stored[micro_index]
        weights_exp = score_exp(query, keys, valid, inv_root)
        d_exp = (
            product("ld,pd->lp", d_numer_low[micro_index], values) + d_denom[micro_index][:, None]
        )
        d_scores = (weights_exp * d_exp).astype(jnp.bfloat16)
        d_values = product(
            "lp,ld->pd", weights_exp.astype(jnp.bfloat16), d_numer_low[micro_index]
        ).astype(jnp.bfloat16)
        d_keys = (product("lp,ld->pd", d_scores, query) * inv_root).astype(jnp.bfloat16)
        query_sum = query_sum + product("lp,pd->ld", d_scores, keys) * inv_root
        key_grad = key_grad + product("pc,pd->cd", pix_low, d_keys)
        value_grad = value_grad + product("pc,pd->cd", pix_low, d_values)
        d_pix_norm = product("pd,cd->pc", d_keys, w_key) + product("pd,cd->pc", d_values, w_value)
        pixel_list.append(pix_back(d_pix_norm * in_gain)[0])
        gain_input = gain_input + jnp.sum(d_pix_norm * pix_std, axis=0)
    pixel_grad = jnp.stack(pixel_list)[:, None]
    lat_resid_full = lax.dynamic_update_slice_in_dim(
        jnp.zeros((LAT, DL), jnp.float32), lat_resid, row_start, 0
    )
    query_total, resid_total, kv_grad, in_gain_grad, gain_mlp_total = lax.psum(
        (query_sum, lat_resid_full, jnp.stack([key_grad, value_grad]), gain_input, gain_mlp),
        ("img", "pix"),
    )
    d_query = query_total.astype(jnp.bfloat16)
    d_lat_norm = product("le,de->ld", d_query, w_query)
    latent_grad = resid_total + lat_norm_back(d_lat_norm * lat_gains[0])[0]
    lat_gain_grad = jnp.stack([jnp.sum(d_lat_norm * lat_norm, axis=0), gain_mlp_total])
    att_rows, branch_rows, hn_rows, hid_rows, act_rows, mlp_rows = row_pairs

    def own_product(left_rows, right_rows):
        return product("mrd,mre->de", left_rows, right_rows)

    grad_query = product("ld,le->de", lat_low, d_query)
    leader = (lax.axis_index(("img", "pix")) == 0).astype(jnp.float32)
    matrices = jnp.stack(
        [
            grad_query * leader,
            own_product(att_rows, branch_rows),
            own_product(hn_rows, hid_rows),
            own_product(act_rows, mlp_rows),
        ]
    )
    buffer = jnp.zeros((NBLK, BLK, BLK), jnp.float32).at[owner].set(to_blocks(matrices, DL, BLK))
    reduced = lax.psum_scatter(buffer, ("img", "pix"), scatter_dimension=0, tiled=True)
    new_left = 0.5 * left_stat + 0.5 * jnp.einsum(
        "bij,bkj->bik", reduced, reduced, precision=HIGHEST_PRECISION
    )
    new_right = 0.5 * right_stat + 0.5 * jnp.einsum(
        "bji,bjk->bik", reduced, reduced, precision=HIGHEST_PRECISION
    )
    half_step = jnp.einsum("bij,bjk->bik", left_root, reduced, precision=HIGHEST_PRECISION)
    shampoo = jnp.einsum("bij,bjk->bik", half_step, right_root, precision=HIGHEST_PRECISION)
    new_master = master - 0.5 / math.sqrt(DL) * normalized(shampoo, (1, 2))
    new_copy = new_master.astype(jnp.bfloat16)
    new_kv = kv_weight - 0.3 / math.sqrt(CIN) * normalized(kv_grad, (1, 2))
    new_latent = latent_array - 0.3 * normalized(latent_grad, (0, 1))
    new_in_gain = in_gain - 0.2 * normalized(in_gain_grad, (0,))
    new_lat_gains = lat_gains - 0.2 * normalized(lat_gain_grad, (1,))
    return (
        latents_out[:, None],
        pixel_grad,
        new_left,
        new_right,
        new_master,
        new_copy,
        kv_grad,
        new_kv,
        latent_grad,
        new_latent,
        in_gain_grad,
        new_in_gain,
        lat_gain_grad,
        new_lat_gains,
    )


def solution(mesh):
    in_specs = (
        P(None, "img", "pix", None),
        P(),
        P(),
        P(("img", "pix"), None, None),
        P(("img", "pix"), None, None),
        P(("img", "pix"), None, None),
        P(("img", "pix"), None, None),
        P(("img", "pix"), None, None),
        P(),
        P(),
        P(),
        P(),
        P(None, "img", "pix", None),
    )
    out_specs = (
        P(None, "img", "pix", None),
        P(None, "img", "pix", None),
        P(("img", "pix"), None, None),
        P(("img", "pix"), None, None),
        P(("img", "pix"), None, None),
        P(("img", "pix"), None, None),
        P(),
        P(),
        P(),
        P(),
        P(),
        P(),
        P(),
        P(),
    )
    return jax.shard_map(shards, mesh=mesh, in_specs=in_specs, out_specs=out_specs, check_vma=False)
```

profile of v0, /device:TPU:0, one launch (start us, length us, event | category | flops | bytes accessed | tf_op | source)
XLA Modules:
  0.0 1375.3 jit_solution(13989832544595955753)
XLA Ops:
  19.6 25.7 %slice_reduce_fusion.1 = (f32[10368]{0:T(1024)S(1)}, f32[10368]{0:T(1024)S(1)}, f32[1,1,10368,261]{2,1,3,0:T(1,128)S(1)}, f32[1,1,10368,261]{2,1,3,0:T(1,128)}) fusion(f32[2,1,10368,261]{2,1,3,0:T(1,128)} %param.13), kind=kLoop, calls=%fused_computation.190 | loop fusion | flops 5391360 | bytes 43379712 | tf_op jit(solution)/shard_map/jvp()/reduce_sum | solution.py:19
  58.2 20.7 %convolution_convert_fusion.4 = bf16[10368,1024]{1,0:T(8,128)(2,1)} fusion(bf16[2,261,1024]{2,1,0:T(8,128)(2,1)} %copy.134, f32[1,1,10368,261]{2,1,3,0:T(1,128)} %copy-done.1, f32[261]{0:T(512)S(1)} %copy-done.47, f32[10368]{0:T(1024)S(1)} %fusion.61, f32[10368]{0:T(1024)S(1)} %broadcast_multiply_fusion.1), kind=kOutput, calls=%fused_computation.13 | convolution fusion | flops 5563427328 | bytes 32682516 | tf_op jit(solution)/shard_map/dot_general | solution.py:137
  78.9 20.8 %convolution_convert_fusion.5 = bf16[10368,1024]{1,0:T(8,128)(2,1)} fusion(bf16[2,261,1024]{2,1,0:T(8,128)(2,1)} %copy.134, f32[1,1,10368,261]{2,1,3,0:T(1,128)} %copy-done.1, f32[261]{0:T(512)S(1)} %copy-done.47, f32[10368]{0:T(1024)S(1)} %fusion.61, f32[10368]{0:T(1024)S(1)} %broadcast_multiply_fusion.1), kind=kOutput, calls=%fused_computation.14 | convolution fusion | flops 5563427328 | bytes 32682516 | tf_op jit(solution)/shard_map/dot_general | solution.py:136
  99.7 20.5 %convolution_convert_fusion.2 = bf16[10368,1024]{1,0:T(8,128)(2,1)} fusion(bf16[2,261,1024]{2,1,0:T(8,128)(2,1)} %copy.134, f32[1,1,10368,261]{2,1,3,0:T(1,128)} %get-tuple-element.87, f32[10368]{0:T(1024)S(1)} %fusion.62, f32[10368]{0:T(1024)S(1)} %broadcast_multiply_fusion, f32[261]{0:T(512)S(1)} %copy-done.47), kind=kOutput, calls=%fused_computation.11 | convolution fusion | flops 5563427328 | bytes 32682516 | tf_op jit(solution)/shard_map/dot_general | solution.py:137
  120.2 20.8 %convolution_convert_fusion.3 = bf16[10368,1024]{1,0:T(8,128)(2,1)} fusion(bf16[2,261,1024]{2,1,0:T(8,128)(2,1)} %copy.134, f32[1,1,10368,261]{2,1,3,0:T(1,128)} %get-tuple-element.87, f32[10368]{0:T(1024)S(1)} %fusion.62, f32[10368]{0:T(1024)S(1)} %broadcast_multiply_fusion, f32[261]{0:T(512)S(1)} %copy-done.47), kind=kOutput, calls=%fused_computation.12 | convolution fusion | flops 5563427328 | bytes 32682516 | tf_op jit(solution)/shard_map/dot_general | solution.py:136
  173.8 20.9 %fusion.85 = (f32[512]{0:T(512)S(1)}, f32[512,10368]{1,0:T(8,128)}) fusion(bf16[512,1024]{1,0:T(8,128)(2,1)S(1)} %fusion.36, bf16[10368,1024]{1,0:T(8,128)(2,1)} %convolution_convert_fusion.5, pred[10368]{0:T(1024)(128)(4,1)S(1)} %get-tuple-element.120), kind=kOutput, calls=%fused_computation.199 | convolution fusion | flops 10887561216 | bytes 43528320 | tf_op jit(solution)/shard_map/ld,pd->lp/dot_general | solution.py:54
  194.7 22.7 %fusion.30 = f32[1,512,1024]{2,1,0:T(8,128)} fusion(bf16[10368,1024]{1,0:T(8,128)(2,1)} %convolution_convert_fusion.4, f32[512,10368]{1,0:T(8,128)} %get-tuple-element.105), kind=kOutput, calls=%fused_computation.109 | convolution fusion | flops 10876944384 | bytes 44564480 | tf_op jit(solution)/shard_map/lp,pd->ld/dot_general | solution.py:54
  217.4 20.8 %fusion.84 = (f32[512]{0:T(512)S(1)}, f32[512,10368]{1,0:T(8,128)}) fusion(bf16[512,1024]{1,0:T(8,128)(2,1)} %copy-done.68, bf16[10368,1024]{1,0:T(8,128)(2,1)} %convolution_convert_fusion.3, pred[10368]{0:T(1024)(128)(4,1)S(1)} %copy-done.60), kind=kOutput, calls=%fused_computation.198 | convolution fusion | flops 10887561216 | bytes 43528320 | tf_op jit(solution)/shard_map/ld,pd->lp/dot_general | solution.py:54
  238.1 22.8 %fusion.33 = f32[1,512,1024]{2,1,0:T(8,128)} fusion(bf16[10368,1024]{1,0:T(8,128)(2,1)} %convolution_convert_fusion.2, f32[512,10368]{1,0:T(8,128)} %get-tuple-element.103), kind=kOutput, calls=%fused_computation.110 | convolution fusion | flops 10876944384 | bytes 44564480 | tf_op jit(solution)/shard_map/lp,pd->ld/dot_general | solution.py:54
  280.2 25.1 %psum.50 = f32[2,512]{1,0:T(2,128)S(1)} all-reduce(f32[2,512]{1,0:T(2,128)S(1)} %pad_maximum_fusion.3), channel_id=1, replica_groups=mesh['img'=4,'pix'=8] {'pix'}, use_global_device_ids=true, to_apply=%region_9.10 | all-reduce | flops 1024 | bytes 8192 | tf_op jit(solution)/shard_map/psum | solution.py:145
  305.4 120.9 %all-reduce.6.cloned.1.call-done = f32[2,512,1024]{2,1,0:T(8,128)} async-done(((f32[2,512,1024]{2,1,0:T(8,128)}), f32[2,512,1024]{2,1,0:T(8,128)}) %all-reduce.6.cloned.1.call-update) | async-done | bytes 4194320 | tf_op jit(solution)/shard_map/psum | solution.py:145
  451.5 25.6 %all-gather.6.cloned.1.call-done = bf16[2,1,512,1024]{3,2,0,1:T(8,128)(2,1)} async-done(((bf16[2,1,64,1024]{3,2,0,1:T(8,128)(2,1)}), bf16[2,1,512,1024]{3,2,0,1:T(8,128)(2,1)}) %all-gather.6.cloned.1.call-update) | async-done | bytes 2097168 | tf_op jit(solution)/shard_map/all_gather | solution.py:146
  502.7 22.3 %convolution_convert_fusion.1 = bf16[10368,1024]{1,0:T(8,128)(2,1)} fusion(f32[512,10368]{1,0:T(8,128)} %get-tuple-element.105, bf16[2,512,1024]{2,1,0:T(8,128)(2,1)S(1)} %get-tuple-element.92), kind=kOutput, calls=%fused_computation.10 | convolution fusion | flops 10887561216 | bytes 43515904 | tf_op jit(solution)/shard_map/lp,ld->pd/dot_general | solution.py:54
  525.0 21.5 %convolution_convert_fusion = bf16[10368,1024]{1,0:T(8,128)(2,1)} fusion(f32[512,10368]{1,0:T(8,128)} %get-tuple-element.103, bf16[2,512,1024]{2,1,0:T(8,128)(2,1)S(1)} %get-tuple-element.92), kind=kOutput, calls=%fused_computation.9 | convolution fusion | flops 10887561216 | bytes 43515904 | tf_op jit(solution)/shard_map/lp,ld->pd/dot_general | solution.py:54
  546.6 22.6 %multiply_convert_fusion.3 = bf16[512,10368]{1,0:T(8,128)(2,1)} fusion(f32[512,10368]{1,0:T(8,128)} %get-tuple-element.105, bf16[10368,1024]{1,0:T(8,128)(2,1)} %convolution_convert_fusion.4, f32[512]{0:T(512)S(1)} %bitcast.234, bf16[2,512,1024]{2,1,0:T(8,128)(2,1)S(1)} %get-tuple-element.92), kind=kOutput, calls=%fused_computation.6 | convolution fusion | flops 10887561216 | bytes 54134784 | tf_op jit(solution)/shard_map/ld,pd->lp/dot_general | solution.py:54
  569.2 19.5 %fusion.88 = f32[512,1024]{1,0:T(8,128)} fusion(bf16[512,10368]{1,0:T(8,128)(2,1)} %multiply_convert_fusion.3, bf16[10368,1024]{1,0:T(8,128)(2,1)} %convolution_convert_fusion.5), kind=kOutput, calls=%fused_computation.202 | convolution fusion | flops 10871635968 | bytes 33947648 | tf_op jit(solution)/shard_map/lp,pd->ld/dot_general | solution.py:54
  588.7 19.0 %multiply_convert_fusion.1 = bf16[10368,1024]{1,0:T(8,128)(2,1)} fusion(bf16[512,10368]{1,0:T(8,128)(2,1)} %multiply_convert_fusion.3, bf16[512,1024]{1,0:T(8,128)(2,1)S(1)} %copy-done.69), kind=kOutput, calls=%fused_computation.3 | convolution fusion | flops 10892869632 | bytes 32899072 | tf_op jit(solution)/shard_map/lp,ld->pd/dot_general | solution.py:54
  607.7 14.2 %fusion.75 = f32[261,1024]{1,0:T(8,128)} fusion(bf16[10368,1024]{1,0:T(8,128)(2,1)} %multiply_convert_fusion.1, f32[1,1,10368,261]{2,1,3,0:T(1,128)} %copy-done.1, f32[10368]{0:T(1024)S(1)} %copy-done.46, f32[261]{0:T(512)S(1)} %copy-done.48, f32[10368]{0:T(1024)S(1)} %copy-done.33), kind=kOutput, calls=%fused_computation.188 | convolution fusion | flops 5552810496 | bytes 33210900 | tf_op jit(solution)/shard_map/pc,pd->cd/dot_general | solution.py:54
  621.9 23.5 %fusion.51 = f32[10368,261]{0,1:T(8,128)} fusion(bf16[10368,1024]{1,0:T(8,128)(2,1)} %multiply_convert_fusion.1, bf16[2,261,1024]{2,1,0:T(8,128)(2,1)S(1)} %copy-done.22), kind=kOutput, calls=%fused_computation.138 | convolution fusion | flops 5541986304 | bytes 32598528 | tf_op jit(solution)/shard_map/pd,cd->pc/dot_general | solution.py:54
  659.9 23.0 %multiply_convert_fusion.2 = bf16[512,10368]{1,0:T(8,128)(2,1)} fusion(f32[512,10368]{1,0:T(8,128)} %get-tuple-element.103, bf16[10368,1024]{1,0:T(8,128)(2,1)} %convolution_convert_fusion.2, f32[512]{0:T(512)S(1)} %bitcast.233, bf16[2,512,1024]{2,1,0:T(8,128)(2,1)} %copy-done.70), kind=kOutput, calls=%fused_computation.5 | convolution fusion | flops 10887561216 | bytes 54134784 | tf_op jit(solution)/shard_map/ld,pd->lp/dot_general | solution.py:54
  682.9 18.4 %multiply_convert_fusion = bf16[10368,1024]{1,0:T(8,128)(2,1)} fusion(bf16[512,10368]{1,0:T(8,128)(2,1)} %multiply_convert_fusion.2, bf16[512,1024]{1,0:T(8,128)(2,1)S(1)} %copy-done.69), kind=kOutput, calls=%fused_computation.2 | convolution fusion | flops 10892869632 | bytes 32899072 | tf_op jit(solution)/shard_map/lp,ld->pd/dot_general | solution.py:54
  701.3 19.9 %add_multiply_fusion = f32[512,1024]{1,0:T(8,128)} fusion(f32[512,1024]{1,0:T(8,128)} %fusion.88, bf16[512,10368]{1,0:T(8,128)(2,1)} %multiply_convert_fusion.2, bf16[10368,1024]{1,0:T(8,128)(2,1)} %convolution_convert_fusion.3), kind=kOutput, calls=%fused_computation.102 | convolution fusion | flops 10872684544 | bytes 36044800 | tf_op jit(solution)/shard_map/lp,pd->ld/dot_general | solution.py:54
  721.3 14.1 %fusion.74 = f32[261,1024]{1,0:T(8,128)} fusion(bf16[10368,1024]{1,0:T(8,128)(2,1)} %convolution_convert_fusion.1, f32[1,1,10368,261]{2,1,3,0:T(1,128)} %copy-done.1, f32[10368]{0:T(1024)S(1)} %copy-done.46, f32[261]{0:T(512)S(1)} %copy-done.48, f32[10368]{0:T(1024)S(1)} %copy-done.33), kind=kOutput, calls=%fused_computation.187 | convolution fusion | flops 5552810496 | bytes 33210900 | tf_op jit(solution)/shard_map/pc,pd->cd/dot_general | solution.py:54
  735.4 28.7 %multiply_reduce_fusion.3 = (f32[10368]{0:T(1024)S(1)}, f32[10368,261]{0,1:T(8,128)}) fusion(f32[1,1,10368,261]{2,1,3,0:T(1,128)} %copy-done.1, f32[261]{0:T(512)S(1)} %copy-done.48, f32[10368]{0:T(1024)S(1)} %copy-done.33, f32[10368,261]{0,1:T(8,128)} %fusion.51, bf16[10368,1024]{1,0:T(8,128)(2,1)} %convolution_convert_fusion.1, ...), kind=kOutput, calls=%fused_computation.29 | convolution fusion | flops 5555505664 | bytes 54335488 | tf_op jit(solution)/shard_map/pd,cd->pc/dot_general | solution.py:54
  764.1 24.0 %fusion.50 = f32[10368,261]{0,1:T(8,128)} fusion(bf16[10368,1024]{1,0:T(8,128)(2,1)} %multiply_convert_fusion, bf16[2,261,1024]{2,1,0:T(8,128)(2,1)S(1)} %copy-done.22), kind=kOutput, calls=%fused_computation.137 | convolution fusion | flops 5541986304 | bytes 32598528 | tf_op jit(solution)/shard_map/pd,cd->pc/dot_general | solution.py:54
  788.2 14.6 %fusion.40 = f32[1,261,1024]{2,1,0:T(8,128)} fusion(f32[261,1024]{1,0:T(8,128)} %fusion.75, bf16[10368,1024]{1,0:T(8,128)(2,1)} %multiply_convert_fusion, f32[1,1,10368,261]{2,1,3,0:T(1,128)} %get-tuple-element.87, f32[10368]{0:T(1024)S(1)} %copy-done.40, f32[261]{0:T(512)S(1)} %copy-done.48, f32[10368]{0:T(1024)S(1)} %copy-done.35), kind=kOutput, calls=%fused_computation.115 | convolution fusion | flops 5553077760 | bytes 34279956 | tf_op jit(solution)/shard_map/pc,pd->cd/dot_general | solution.py:54
  814.9 28.8 %multiply_reduce_fusion.1 = (f32[261]{0:T(512)S(1)}, f32[10368]{0:T(1024)S(1)}, f32[10368]{0:T(1024)S(1)}, f32[10368,261]{0,1:T(8,128)}) fusion(f32[10368,261]{0,1:T(8,128)} %get-tuple-element.112, f32[1,1,10368,261]{2,1,3,0:T(1,128)} %copy-done.1, f32[10368]{0:T(1024)S(1)} %copy-done.46, f32[10368]{0:T(1024)S(1)} %copy-done.33, ...), kind=kOutput, calls=%fused_computation.23 | convolution fusion | flops 5582555648 | bytes 76161552 | tf_op jit(solution)/shard_map/pd,cd->pc/dot_general | solution.py:54
  859.1 76.5 %all-reduce.9 = (bf16[512,1024]{1,0:T(8,128)(2,1)}, f32[261]{0:T(512)S(1)}, f32[1,1024]{1,0:T(1,128)S(1)}) all-reduce(f32[512,1024]{1,0:T(8,128)} %add_multiply_fusion, f32[261]{0:T(512)S(1)} %add.229, f32[1,1024]{1,0:T(1,128)S(1)} %bitcast.225), channel_id=1, replica_groups=mesh['img'=4,'pix'=8] {'img','pix'}, use_global_device_ids=true, to_apply=%region_19.20 | all-reduce | flops 525573 | bytes 3156008 | tf_op jit(solution)/shard_map/psum | solution.py:189
  957.8 45.9 %scatter_fusion = f32[256,128,128]{2,1,0:T(8,128)} fusion(f32[256,128,128]{2,1,0:T(8,128)} %broadcast_in_dim.117, s32[256]{0:T(256)S(1)} %copy-done.62, f32[256,128,128]{2,1,0:T(8,128)} %bitcast.213), kind=kCustom, calls=%fused_computation.1 | custom fusion | bytes 50332672 | tf_op jit(solution)/shard_map/scatter | solution.py:212
  1005.1 24.9 %add_bitcast_fusion.1 = (f32[1,10368,261]{1,2,0:T(8,128)}, f32[1,10368,261]{1,2,0:T(8,128)}) fusion(f32[10368]{0:T(1024)S(1)} %negate_multiply_fusion.2, f32[10368]{0:T(1024)S(1)} %multiply_multiply_fusion.6, f32[10368]{0:T(1024)S(1)} %copy-done.33, f32[1,1,10368,261]{2,1,3,0:T(1,128)} %copy-done.1, f32[10368]{0:T(1024)S(1)} %copy-done.46, ...), kind=kLoop, calls=%fused_computation.28 | loop fusion | flops 37884672 | bytes 65277972 | tf_op jit(solution)/shard_map/stack | solution.py:185
  1038.5 27.0 %copy.60 = f32[2,1,10368,261]{2,1,3,0:T(1,128)} copy(f32[2,1,10368,261]{2,3,0,1:T(8,128)S(1)} %maximum_bitcast_fusion) | data formatting | bytes 43296768
  1091.2 269.6 %reduce-scatter.2.cloned.1.call-done = f32[8,128,128]{2,1,0:T(8,128)} async-done(((f32[256,128,128]{2,1,0:T(8,128)}), f32[8,128,128]{2,1,0:T(8,128)}) %reduce-scatter.2.cloned.1.call-update) | async-done | bytes 524304 | tf_op jit(solution)/shard_map/reduce_scatter | solution.py:213
  (255 shorter events, 230.9 us)
Async XLA Ops:
  7.2 1355.5 %copy-start = (f32[8,128,128]{2,1,0:T(8,128)S(1)}, f32[8,128,128]{2,1,0:T(8,128)}, u32[]{:S(2)}) copy-start(f32[8,128,128]{2,1,0:T(8,128)} %param.20) | copy-start | bytes 1572868
  7.2 133.8 %all-gather.4.cloned.1.call-start = ((), (), s32[]{:S(2)}) async-start(), calls=%async_computation.1 | async-start | bytes 8650752 | tf_op jit(solution)/shard_map/all_gather | solution.py:121
  9.2 417.1 %all-reduce.6.cloned.1.call-start = ((), (), s32[]{:S(2)}) async-start(), calls=%async_computation.2 | async-start | bytes 8388608 | tf_op jit(solution)/shard_map/psum | solution.py:145
  18.0 153.1 %copy-start.53 = (f32[512]{0:T(512)}, f32[512]{0:T(512)S(1)}, u32[]{:S(2)}) copy-start(f32[512]{0:T(512)S(1)} %broadcast_multiply_fusion.3) | copy-start | bytes 6148
  18.3 26.9 %copy-start.55 = (f32[512]{0:T(512)}, f32[512]{0:T(512)S(1)}, u32[]{:S(2)}) copy-start(f32[512]{0:T(512)S(1)} %multiply_reduce_fusion.12) | copy-start | bytes 6148
  18.4 152.7 %copy-start.63 = (f32[512]{0:T(512)}, f32[512]{0:T(512)S(1)}, u32[]{:S(2)}) copy-start(f32[512]{0:T(512)S(1)} %fusion.67) | copy-start | bytes 6148
  19.0 152.1 %copy-start.58 = (f32[1,1024]{1,0:T(1,128)}, f32[1,1024]{1,0:T(1,128)S(1)}, u32[]{:S(2)}) copy-start(f32[1,1024]{1,0:T(1,128)S(1)} %get-tuple-element.94) | copy-start | bytes 12292
  45.3 33.6 %copy-start.32 = (f32[10368]{0:T(1024)}, f32[10368]{0:T(1024)S(1)}, u32[]{:S(2)}) copy-start(f32[10368]{0:T(1024)S(1)} %broadcast_multiply_fusion.1) | copy-start | bytes 124420
  45.3 74.9 %copy-start.34 = (f32[10368]{0:T(1024)}, f32[10368]{0:T(1024)S(1)}, u32[]{:S(2)}) copy-start(f32[10368]{0:T(1024)S(1)} %broadcast_multiply_fusion) | copy-start | bytes 124420
  58.1 62.1 %copy-start.39 = (f32[10368]{0:T(1024)}, f32[10368]{0:T(1024)S(1)}, u32[]{:S(2)}) copy-start(f32[10368]{0:T(1024)S(1)} %fusion.62) | copy-start | bytes 124420
  194.7 22.7 %copy-start.60 = (pred[10368]{0:T(1024)(128)(4,1)S(1)}, pred[10368]{0:T(1024)(128)(4,1)}, u32[]{:S(2)}) copy-start(pred[10368]{0:T(1024)(128)(4,1)} %get-tuple-element.119) | copy-start | bytes 31108
  265.8 211.3 %all-gather.6.cloned.1.call-start = ((), (), s32[]{:S(2)}) async-start(), calls=%async_computation.4 | async-start | bytes 2359296 | tf_op jit(solution)/shard_map/all_gather | solution.py:146
  267.6 807.7 %all-reduce.8.cloned.1.call-start = ((), (), s32[]{:S(2)}) async-start(), calls=%async_computation.5 | async-start | bytes 8519680 | tf_op jit(solution)/shard_map/psum | solution.py:189
  502.7 43.8 %copy-start.70 = (bf16[2,512,1024]{2,1,0:T(8,128)(2,1)}, bf16[2,512,1024]{2,1,0:T(8,128)(2,1)S(1)}, u32[]{:S(2)}) copy-start(bf16[2,512,1024]{2,1,0:T(8,128)(2,1)S(1)} %get-tuple-element.92) | copy-start | bytes 6291460
  735.4 28.7 %copy-start.44 = (f32[10368]{0:T(1024)S(1)}, f32[10368]{0:T(1024)}, u32[]{:S(2)}) copy-start(f32[10368]{0:T(1024)} %copy-done.43) | copy-start | bytes 124420
  764.1 24.1 %copy-start.35 = (f32[10368]{0:T(1024)S(1)}, f32[10368]{0:T(1024)}, u32[]{:S(2)}) copy-start(f32[10368]{0:T(1024)} %copy-done.34) | copy-start | bytes 124420
  764.1 24.1 %copy-start.40 = (f32[10368]{0:T(1024)S(1)}, f32[10368]{0:T(1024)}, u32[]{:S(2)}) copy-start(f32[10368]{0:T(1024)} %copy-done.39) | copy-start | bytes 124420
  764.1 38.6 %slice-start = ((s8[10824192]{0:T(1024)(128)(4,1)}), s8[4194304]{0:T(1024)(128)(4,1)S(1)}, s32[]{:S(2)}) async-start(s8[10824192]{0:T(1024)(128)(4,1)} %bitcast.211), calls=%async_computation.6 | async-start | bytes 8388608
  764.1 38.6 %slice-start.1 = ((s8[10824192]{0:T(1024)(128)(4,1)}), s8[4194304]{0:T(1024)(128)(4,1)S(1)}, s32[]{:S(2)}) async-start(s8[10824192]{0:T(1024)(128)(4,1)} %bitcast.211), calls=%async_computation.7 | async-start | bytes 8388608
  814.9 28.8 %copy-start.42 = (f32[10368]{0:T(1024)S(1)}, f32[10368]{0:T(1024)}, u32[]{:S(2)}) copy-start(f32[10368]{0:T(1024)} %copy-done.41) | copy-start | bytes 124420
  814.9 29.1 %copy-start.31 = (f32[64,1024]{1,0:T(8,128)S(1)}, f32[64,1024]{1,0:T(8,128)}, u32[]{:S(2)}) copy-start(f32[64,1024]{1,0:T(8,128)} %dynamic-slice_reduce_fusion) | copy-start | bytes 786436
  848.1 512.7 %reduce-scatter.2.cloned.1.call-start = ((), (), s32[]{:S(2)}) async-start(), calls=%async_computation.3 | async-start | bytes 17301504 | tf_op jit(solution)/shard_map/reduce_scatter | solution.py:213
  848.1 87.5 %copy-start.5 = (f32[512,1024]{1,0:T(8,128)S(1)}, f32[512,1024]{1,0:T(8,128)}, u32[]{:S(2)}) copy-start(f32[512,1024]{1,0:T(8,128)} %param.22) | copy-start | bytes 6291460
  848.1 87.4 %copy-start.54 = (f32[512]{0:T(512)S(1)}, f32[512]{0:T(512)}, u32[]{:S(2)}) copy-start(f32[512]{0:T(512)} %copy-done.53) | copy-start | bytes 6148
  848.2 87.4 %copy-start.59 = (f32[1,1024]{1,0:T(1,128)S(1)}, f32[1,1024]{1,0:T(1,128)}, u32[]{:S(2)}) copy-start(f32[1,1024]{1,0:T(1,128)} %copy-done.58) | copy-start | bytes 12292
  848.2 87.4 %copy-start.64 = (f32[512]{0:T(512)S(1)}, f32[512]{0:T(512)}, u32[]{:S(2)}) copy-start(f32[512]{0:T(512)} %copy-done.63) | copy-start | bytes 6148
  935.6 138.4 %copy-start.65 = (f32[261]{0:T(512)}, f32[261]{0:T(512)S(1)}, u32[]{:S(2)}) copy-start(f32[261]{0:T(512)S(1)} %get-tuple-element.68) | copy-start | bytes 3136
  1038.5 27.0 %copy-start.30 = (bf16[1,8,128,8,128]{4,3,2,1,0:T(8,128)(2,1)S(1)}, bf16[1,8,128,8,128]{4,3,2,1,0:T(8,128)(2,1)}, u32[]{:S(2)}) copy-start(bf16[1,8,128,8,128]{4,3,2,1,0:T(8,128)(2,1)} %copy-done.29) | copy-start | bytes 6291460
  1038.5 27.0 %copy-start.67 = (bf16[512,1024]{1,0:T(8,128)(2,1)S(1)}, bf16[512,1024]{1,0:T(8,128)(2,1)}, u32[]{:S(2)}) copy-start(bf16[512,1024]{1,0:T(8,128)(2,1)} %get-tuple-element.67) | copy-start | bytes 3145732
  1089.5 274.0 %copy-start.28 = (f32[8,128,128]{2,1,0:T(8,128)S(1)}, f32[8,128,128]{2,1,0:T(8,128)}, u32[]{:S(2)}) copy-start(f32[8,128,128]{2,1,0:T(8,128)} %param.16) | copy-start | bytes 1572868
  1091.2 273.2 %copy-start.37 = (f32[8,128,128]{2,1,0:T(8,128)S(1)}, f32[8,128,128]{2,1,0:T(8,128)}, u32[]{:S(2)}) copy-start(f32[8,128,128]{2,1,0:T(8,128)} %param.18) | copy-start | bytes 1572868
  1091.2 275.1 %copy-start.38 = (f32[8,128,128]{2,1,0:T(8,128)S(1)}, f32[8,128,128]{2,1,0:T(8,128)}, u32[]{:S(2)}) copy-start(f32[8,128,128]{2,1,0:T(8,128)} %param.17) | copy-start | bytes 1572868
  (47 other events, 334.8 us)
Sparse Core Ops, SparseCore 0:
  11.6 79.8 all-gather.3
  265.9 160.3 all-reduce.5
  429.1 48.0 all-gather.5
  848.2 143.0 all-reduce.7
  1003.9 356.8 reduce-scatter.1
where the time goes:
time: 1390 us; the launch traced here: 1380 us
  matrix products  539 us (39%)
  waiting for transfers between devices  416 us (30%)
  local copies, waits for them, and re-layouts  151 us (11%)
  other arithmetic  148 us (11%)
  blocking collectives  102 us (7%)
  between operations  19.1 us (1%)
    dot_general x31, matrix products, product(): jnp.einsum(pattern, left_side, right_side, preferred_element_type=jnp.flo...  449 us
    reduce_scatter x1, waiting for transfers between devices, shards(): lax.psum_scatter(buffer, ('img', 'pix'), scatter_dimension=0, tiled=True)  270 us
    psum x1, waiting for transfers between devices, shards(): numer_all, denom_all = lax.psum((numerator, denominator), 'pix')  121 us
    psum x1, blocking collectives, shards(): lax.psum((query_sum, lat_resid_full, jnp.stack([key_grad, value_grad]), g...  76.5 us
    unnamed x156, local copies, waits for them, and re-layouts  57.4 us
    scatter x1, local copies, waits for them, and re-layouts, shards(): jnp.zeros((NBLK, BLK, BLK), jnp.float32).at[owner]  45.9 us
    dot_general x2, matrix products, shards(): jnp.dot(pix_low, w_key, preferred_element_type=jnp.float32)  41.7 us
    dot_general x2, matrix products, shards(): jnp.dot(pix_low, w_value, preferred_element_type=jnp.float32)  41.2 us
  transfers between devices with their start and end apart: 5, of which 3 were waited for; matrix products, arithmetic and copies ran while one was open for 24% of the time, Pallas kernels for 0%

commit v1 on v0

--- a/solution.py
+++ b/solution.py
@@ -54,14 +54,7 @@
     return jnp.einsum(pattern, left_side, right_side, preferred_element_type=jnp.float32)
 
 
-def score_exp(query, keys, valid, inv_root):
-    scores = product("ld,pd->lp", query, keys) * inv_root
-    return jnp.where(valid[None, :], jnp.exp(scores), 0.0)
-
-
-def latent_pass(
-    numerator, denominator, lat_part, cot_rows, own_start, own_count, lat_gain, w_out, w_up, w_down
-):
+def latent_pass(numerator, denominator, lat_part, cot_rows, lat_gain, w_out, w_up, w_down):
     attended = numerator / denominator[..., None]
     att_low = attended.astype(jnp.bfloat16)
     resid = lat_part[None] + product("mrd,de->mre", att_low, w_out)
@@ -80,21 +73,19 @@
     d_attended = product("mre,de->mrd", d_branch, w_out)
     d_numer = d_attended / denominator[..., None]
     d_denom = -jnp.sum(d_attended * numerator / (denominator * denominator)[..., None], axis=-1)
-
-    def own_rows(array):
-        return lax.dynamic_slice_in_dim(array, own_start, own_count, 1)
-
-    row_pairs = (
-        own_rows(att_low),
-        own_rows(d_branch),
-        own_rows(hn_low),
-        own_rows(d_hidden),
-        own_rows(act_low),
-        own_rows(g_mlp),
-    )
-    gain_mlp = jnp.sum(own_rows(d_normed * normed), axis=(0, 1))
-    lat_resid = jnp.sum(own_rows(d_resid), axis=0)
-    return (own_rows(latents_out), d_numer, d_denom, (row_pairs, gain_mlp, lat_resid))
+    row_pairs = (att_low, d_branch, hn_low, d_hidden, act_low, g_mlp)
+    gain_mlp = jnp.sum(d_normed * normed, axis=(0, 1))
+    lat_resid = jnp.sum(d_resid, axis=0)
+    return (latents_out, d_numer.astype(jnp.bfloat16), d_denom, (row_pairs, gain_mlp, lat_resid))
+
+
+def fine(pattern, left_side, right_side):
+    return jnp.einsum(
+        pattern,
+        left_side.astype(jnp.float32),
+        right_side.astype(jnp.float32),
+        precision=HIGHEST_PRECISION,
+    )
 
 
 def shards(
@@ -126,6 +117,7 @@
     lat_norm, lat_norm_back = jax.vjp(standardize, latent_array)
     lat_low = (lat_norm * lat_gains[0]).astype(jnp.bfloat16)
     query = jnp.dot(lat_low, w_query, preferred_element_type=jnp.float32).astype(jnp.bfloat16)
+    query_in = (product("ld,cd->lc", query, w_key) * inv_root).astype(jnp.bfloat16)
     positions = pix_start + jnp.arange(rows_dev, dtype=jnp.int32)
     stored = []
     numer_list = []
@@ -133,64 +125,56 @@
     for micro_index in range(micro):
         pix_std, pix_back = jax.vjp(standardize, pixels[micro_index, 0])
         pix_low = (pix_std * in_gain).astype(jnp.bfloat16)
-        keys = jnp.dot(pix_low, w_key, preferred_element_type=jnp.float32).astype(jnp.bfloat16)
-        values = jnp.dot(pix_low, w_value, preferred_element_type=jnp.float32).astype(jnp.bfloat16)
         valid = positions < sides[micro_index] * sides[micro_index]
-        weights_exp = score_exp(query, keys, valid, inv_root)
-        numer_list.append(product("lp,pd->ld", weights_exp.astype(jnp.bfloat16), values))
+        scores = product("lc,pc->lp", query_in, pix_low)
+        weights_exp = jnp.where(valid[None, :], jnp.exp(scores), 0.0)
+        numer_list.append(product("lp,pc->lc", weights_exp.astype(jnp.bfloat16), pix_low))
         denom_list.append(jnp.sum(weights_exp, axis=1))
-        stored.append((pix_std, pix_back, pix_low, keys, values, valid))
-    numerator = jnp.stack(numer_list)
-    denominator = jnp.stack(denom_list)
-    numer_all, denom_all = lax.psum((numerator, denominator), "pix")
-    cot_all = lax.all_gather(
-        cotangent[:, 0].astype(jnp.bfloat16), "pix", axis=1, tiled=True
-    ).astype(jnp.float32)
+        stored.append((pix_std, pix_back, pix_low, valid))
+    numer_in = lax.psum_scatter(jnp.stack(numer_list), "pix", scatter_dimension=1, tiled=True)
+    denominator = lax.psum_scatter(jnp.stack(denom_list), "pix", scatter_dimension=1, tiled=True)
+    numerator = fine("mlc,cd->mld", numer_in, w_value)
     latents_out, d_numer, d_denom, latent_grads = latent_pass(
-        numer_all,
-        denom_all,
-        latent_array,
-        cot_all,
-        row_start,
-        lat_rows,
+        numerator,
+        denominator,
+        lax.dynamic_slice_in_dim(latent_array, row_start, lat_rows, 0),
+        cotangent[:, 0],
         lat_gains[1],
         w_out,
         w_up,
         w_down,
     )
     row_pairs, gain_mlp, lat_resid = latent_grads
-    d_numer_low = d_numer.astype(jnp.bfloat16)
-    query_sum = jnp.zeros((LAT, DL), jnp.float32)
-    key_grad = jnp.zeros((CIN, DL), jnp.float32)
-    value_grad = jnp.zeros((CIN, DL), jnp.float32)
+    value_grad = fine("mlc,mld->cd", numer_in, d_numer)
+    d_numer_in = product("mld,cd->mlc", d_numer, w_value).astype(jnp.bfloat16)
+    d_numer_all = lax.all_gather(d_numer_in, "pix", axis=1, tiled=True)
+    d_denom_all = lax.all_gather(d_denom, "pix", axis=1, tiled=True)
+    score_sum = jnp.zeros((LAT, CIN), jnp.float32)
     gain_input = jnp.zeros((CIN,), jnp.float32)
     pixel_list = []
     for micro_index in range(micro):
-        pix_std, pix_back, pix_low, keys, values, valid = stored[micro_index]
-        weights_exp = score_exp(query, keys, valid, inv_root)
-        d_exp = (
-            product("ld,pd->lp", d_numer_low[micro_index], values) + d_denom[micro_index][:, None]
+        pix_std, pix_back, pix_low, valid = stored[micro_index]
+        scores = product("lc,pc->lp", query_in, pix_low)
+        weights_exp = jnp.where(valid[None, :], jnp.exp(scores), 0.0)
+        d_exp = product("lc,pc->lp", d_numer_all[micro_index], pix_low) + d_denom_all[micro_index][:, None]
+        d_scores = (weights_exp * d_exp).astype(jnp.bfloat16)
+        score_sum = score_sum + product("lp,pc->lc", d_scores, pix_low)
+        d_pix_norm = product("lp,lc->pc", d_scores, query_in) + product(
+            "lp,lc->pc", weights_exp.astype(jnp.bfloat16), d_numer_all[micro_index]
         )
-        d_scores = (weights_exp * d_exp).astype(jnp.bfloat16)
-        d_values = product(
-            "lp,ld->pd", weights_exp.astype(jnp.bfloat16), d_numer_low[micro_index]
-        ).astype(jnp.bfloat16)
-        d_keys = (product("lp,ld->pd", d_scores, query) * inv_root).astype(jnp.bfloat16)
-        query_sum = query_sum + product("lp,pd->ld", d_scores, keys) * inv_root
-        key_grad = key_grad + product("pc,pd->cd", pix_low, d_keys)
-        value_grad = value_grad + product("pc,pd->cd", pix_low, d_values)
-        d_pix_norm = product("pd,cd->pc", d_keys, w_key) + product("pd,cd->pc", d_values, w_value)
         pixel_list.append(pix_back(d_pix_norm * in_gain)[0])
         gain_input = gain_input + jnp.sum(d_pix_norm * pix_std, axis=0)
     pixel_grad = jnp.stack(pixel_list)[:, None]
     lat_resid_full = lax.dynamic_update_slice_in_dim(
         jnp.zeros((LAT, DL), jnp.float32), lat_resid, row_start, 0
     )
-    query_total, resid_total, kv_grad, in_gain_grad, gain_mlp_total = lax.psum(
-        (query_sum, lat_resid_full, jnp.stack([key_grad, value_grad]), gain_input, gain_mlp),
+    score_total, resid_total, value_total, in_gain_grad, gain_mlp_total = lax.psum(
+        (score_sum, lat_resid_full, value_grad, gain_input, gain_mlp),
         ("img", "pix"),
     )
-    d_query = query_total.astype(jnp.bfloat16)
+    d_query = (fine("lc,cd->ld", score_total, w_key) * inv_root).astype(jnp.bfloat16)
+    key_total = fine("lc,ld->cd", score_total, query) * inv_root
+    kv_grad = jnp.stack([key_total, value_total])
     d_lat_norm = product("le,de->ld", d_query, w_query)
     latent_grad = resid_total + lat_norm_back(d_lat_norm * lat_gains[0])[0]
     lat_gain_grad = jnp.stack([jnp.sum(d_lat_norm * lat_norm, axis=0), gain_mlp_total])

time: 1390 us -> 1040 us (0.75)
  matrix products: 539 us -> 202 us
  other arithmetic: 148 us -> 127 us
  waiting for transfers between devices: 416 us -> 431 us
    dot_general x31 -> x25, matrix products: 449 us -> 184 us  [product(): jnp.einsum(pattern, left_side, right_side, preferred_element_type=jnp.flo...]
    unnamed x5 -> x7, waiting for transfers between devices: 0.08 us -> 131 us
    reduce_scatter x1, waiting for transfers between devices: 270 us -> 153 us  [shards(): lax.psum_scatter(buffer, ('img', 'pix'), scatter_dimension=0, tiled=True)]
    dot_general x4, matrix products: 82.9 us -> 7.37 us  [fine(): jnp.einsum(pattern, left_side.astype(jnp.float32), right_side.astype(jnp....]
    psum x2 -> x1, blocking collectives: 102 us -> 44.9 us  [shards(): lax.psum((score_sum, lat_resid_full, value_grad, gain_input, gain_mlp), (...]
    all_gather x0 -> x2, blocking collectives: none -> 53.4 us  [the longest x1 34.5 us: shards(): d_numer_all = lax.all_gather(d_numer_in, 'pix', axis=1, tiled=True)]
    all_gather x1 -> x0, waiting for transfers between devices: 25.6 us -> none  [shards(): lax.all_gather(cotangent[:, 0].astype(jnp.bfloat16), 'pix', axis=1, tiled...]
    all_gather x1, waiting for transfers between devices: 0.01 us -> 23.5 us  [shards(): lax.all_gather(master.astype(jnp.bfloat16), ('img', 'pix'), axis=0, tiled...]
  transfers between devices with their start and end apart: 5 -> 5, of which waited for: 3 -> 5; matrix products, arithmetic and copies ran while one was open for 24% -> 24% of each run, Pallas kernels for 0% -> 0%
where the time goes in v1:
time: 1040 us; the launch traced here: 1030 us
  waiting for transfers between devices  431 us (41%)
  matrix products  202 us (19%)
  local copies, waits for them, and re-layouts  153 us (15%)
  other arithmetic  127 us (12%)
  blocking collectives  98.3 us (9%)
  between operations  19.9 us (2%)
    dot_general x25, matrix products, product(): jnp.einsum(pattern, left_side, right_side, preferred_element_type=jnp.flo...  184 us
    reduce_scatter x1, waiting for transfers between devices, shards(): lax.psum_scatter(buffer, ('img', 'pix'), scatter_dimension=0, tiled=True)  153 us
    unnamed x7, waiting for transfers between devices  131 us
    psum x1, waiting for transfers between devices, shards(): lax.psum((score_sum, lat_resid_full, value_grad, gain_input, gain_mlp), (...  123 us
    unnamed x167, local copies, waits for them, and re-layouts  52.1 us
    scatter x1, local copies, waits for them, and re-layouts, shards(): jnp.zeros((NBLK, BLK, BLK), jnp.float32).at[owner]  45.5 us
    psum x1, blocking collectives, shards(): lax.psum((score_sum, lat_resid_full, value_grad, gain_input, gain_mlp), (...  44.9 us
    all_gather x1, blocking collectives, shards(): d_numer_all = lax.all_gather(d_numer_in, 'pix', axis=1, tiled=True)  34.5 us
  transfers between devices with their start and end apart: 5, of which 5 were waited for; matrix products, arithmetic and copies ran while one was open for 24% of the time, Pallas kernels for 0%

profile of v1, /device:TPU:0, one launch (start us, length us, event | category | flops | bytes accessed | tf_op | source)
XLA Modules:
  0.0 1032.2 jit_solution(2373091212825880201)
XLA Ops:
  22.7 25.6 %slice_reduce_fusion.1 = (f32[10368]{0:T(1024)S(1)}, f32[10368]{0:T(1024)S(1)}, f32[1,1,10368,261]{2,1,3,0:T(1,128)S(1)}, f32[1,1,10368,261]{2,1,3,0:T(1,128)}) fusion(f32[2,1,10368,261]{2,1,3,0:T(1,128)} %param.13), kind=kLoop, calls=%fused_computation.202 | loop fusion | flops 5391360 | bytes 43379712 | tf_op jit(solution)/shard_map/jvp()/reduce_sum | solution.py:19
  48.4 12.3 %multiply_reduce_fusion.4 = (f32[10368]{0:T(1024)S(1)}, f32[10368]{0:T(1024)S(1)}) fusion(f32[1,1,10368,261]{2,1,3,0:T(1,128)} %get-tuple-element.85, f32[10368]{0:T(1024)S(1)} %broadcast_multiply_fusion, f32[10368]{0:T(1024)S(1)} %broadcast_multiply_fusion.1, f32[1,1,10368,261]{2,1,3,0:T(1,128)S(1)} %get-tuple-element.84), kind=kLoop, calls=%fused_computation.23 | loop fusion | flops 16215552 | bytes 21814272 | tf_op jit(solution)/shard_map/jvp()/reduce_sum | solution.py:21
  62.0 5.9 multiply_convert_fusion.5
  67.9 23.5 %all-gather.3.cloned.1.call-done = bf16[256,128,128]{2,1,0:T(8,128)(2,1)} async-done(((bf16[8,128,128]{2,1,0:T(8,128)(2,1)}), bf16[256,128,128]{2,1,0:T(8,128)(2,1)}) %all-gather.3.cloned.1.call-update) | async-done | bytes 8388624 | tf_op jit(solution)/shard_map/all_gather | solution.py:112
  91.4 12.6 %gather_fusion = bf16[256,128,128]{2,1,0:T(8,128)(2,1)} fusion(bf16[256,128,128]{2,1,0:T(8,128)(2,1)} %all-gather.3.cloned.1.call-done, s32[1024]{0:T(1024)S(1)} %pad_clamp_fusion), kind=kCustom, calls=%fused_computation | custom fusion | bytes 16778240 | tf_op jit(solution)/shard_map/jit(_take)/gather | solution.py:113
  104.0 12.0 %fusion = bf16[4,8,128,8,128]{4,3,2,1,0:T(8,128)(2,1)} fusion(bf16[4,8,8,128,128]{4,3,2,1,0:T(8,128)(2,1)} %bitcast.278, pred[4,8,8]{2,1,0:T(8,128)(4,1)S(1)} %broadcast_in_dim.103), kind=kLoop, calls=%fused_computation.27 | loop fusion | flops 4194304 | bytes 16777472 | tf_op jit(solution)/shard_map/transpose | solution.py:33
  125.6 11.8 %fusion.92 = (f32[512]{0:T(512)S(1)}, f32[512,10368]{1,0:T(8,128)}) fusion(bf16[512,261]{0,1:T(8,128)(2,1)S(1)} %fusion.36, bf16[10368,261]{0,1:T(8,128)(2,1)S(1)} %bitcast.275, pred[10368]{0:T(1024)(128)(4,1)S(1)} %get-tuple-element.121), kind=kOutput, calls=%fused_computation.210 | convolution fusion | flops 2781609472 | bytes 26925440 | tf_op jit(solution)/shard_map/lc,pc->lp/dot_general | solution.py:54
  137.3 9.8 fusion.30
  147.1 11.6 %fusion.93 = (f32[512]{0:T(512)S(1)}, f32[512,10368]{1,0:T(8,128)}) fusion(bf16[512,261]{0,1:T(8,128)(2,1)S(1)} %fusion.36, bf16[10368,261]{0,1:T(8,128)(2,1)S(1)} %bitcast.277, pred[10368]{0:T(1024)(128)(4,1)S(1)} %get-tuple-element.122), kind=kOutput, calls=%fused_computation.211 | convolution fusion | flops 2781609472 | bytes 26925440 | tf_op jit(solution)/shard_map/lc,pc->lp/dot_general | solution.py:54
  158.7 9.6 fusion.27
  189.4 40.6 %reduce-scatter.7.cloned.1.call-done = f32[64,2]{1,0:T(8,128)} async-done(((f32[512,2]{1,0:T(8,128)}), f32[64,2]{1,0:T(8,128)}) %reduce-scatter.7.cloned.1.call-update) | async-done | bytes 528
  231.4 90.5 %all-reduce.6.cloned.1.call-done = f32[2,512,261]{2,0,1:T(2,128)} async-done(((f32[2,512,261]{2,0,1:T(2,128)}), f32[2,512,261]{2,0,1:T(2,128)}) %all-reduce.6.cloned.1.call-update) | async-done | bytes 1069072
  339.8 18.8 %all-gather = f32[8,64,2]{1,2,0:T(2,128)S(1)} all-gather(f32[1,64,2]{1,2,0:T(2,128)S(1)} %negate_bitcast_fusion), channel_id=1, replica_groups=mesh['img'=4,'pix'=8] {'pix'}, dimensions={0}, use_global_device_ids=true | all-gather | bytes 4608 | tf_op jit(solution)/shard_map/all_gather | solution.py:151
  362.0 34.5 %all_gather.10 = bf16[2,512,261]{2,1,0:T(8,128)(2,1)} all-gather(bf16[2,64,261]{2,1,0:T(8,128)(2,1)} %convolution_convert_fusion), channel_id=1, replica_groups=mesh['img'=4,'pix'=8] {'pix'}, dimensions={1}, use_global_device_ids=true | all-gather | bytes 601344 | tf_op jit(solution)/shard_map/all_gather | solution.py:150
  396.5 16.9 %multiply_convert_fusion.1 = bf16[512,10368]{1,0:T(8,128)(2,1)} fusion(f32[512,10368]{1,0:T(8,128)} %get-tuple-element.106, f32[512]{0:T(512)} %bitcast.292, f32[1,1,10368,261]{2,1,3,0:T(1,128)} %copy-done.1, f32[261]{0:T(512)S(1)} %copy-done.43, f32[10368]{0:T(1024)S(1)} %fusion.76, f32[10368]{0:T(1024)S(1)} %broadcast_multiply_fusion.1, ...), kind=kOutput, calls=%fused_computation.4 | convolution fusion | flops 2797742592 | bytes 43153940 | tf_op jit(solution)/shard_map/lc,pc->lp/dot_general | solution.py:54
  413.4 16.7 %multiply_convert_fusion = bf16[512,10368]{1,0:T(8,128)(2,1)} fusion(f32[512,10368]{1,0:T(8,128)} %get-tuple-element.104, f32[512]{0:T(512)} %bitcast.291, f32[1,1,10368,261]{2,1,3,0:T(1,128)} %get-tuple-element.85, f32[10368]{0:T(1024)} %copy-done.29, f32[10368]{0:T(1024)S(1)} %broadcast_multiply_fusion, f32[261]{0:T(512)S(1)} %copy-done.43, ...), kind=kOutput, calls=%fused_computation.3 | convolution fusion | flops 2797742592 | bytes 43157524 | tf_op jit(solution)/shard_map/lc,pc->lp/dot_general | solution.py:54
  430.1 7.8 fusion.97
  438.8 6.3 convolution_add_fusion.6
  463.1 123.2 %all-reduce.8.cloned.1.call-done = (f32[512,261]{0,1:T(8,128)}, f32[1,261,1024]{2,1,0:T(8,128)}, f32[512,1024]{1,0:T(8,128)}) async-done(((f32[512,261]{0,1:T(8,128)}, f32[1,261,1024]{2,1,0:T(8,128)}, f32[512,1024]{1,0:T(8,128)}), (f32[512,261]{0,1:T(8,128)}, f32[1,261,1024]{2,1,0:T(8,128)}, f32[512,1024]{1,0:T(8,128)})) %all-reduce.8.cloned.1.call-update) | async-done | bytes 3700752 | tf_op jit(solution)/shard_map/psum | solution.py:171
  596.3 6.2 pad_maximum_fusion
  602.4 8.0 broadcast_in_dim.117
  610.4 45.5 %scatter_fusion = f32[256,128,128]{2,1,0:T(8,128)} fusion(f32[256,128,128]{2,1,0:T(8,128)} %broadcast_in_dim.117, s32[256]{0:T(256)S(1)} %copy-done.61, f32[256,128,128]{2,1,0:T(8,128)} %bitcast.273), kind=kCustom, calls=%fused_computation.1 | custom fusion | bytes 50332672 | tf_op jit(solution)/shard_map/scatter | solution.py:196
  655.9 9.8 fusion.95
  665.8 20.8 %multiply_reduce_fusion.3 = (f32[10368]{0:T(1024)S(1)}, f32[10368,261]{0,1:T(8,128)}) fusion(f32[1,1,10368,261]{2,1,3,0:T(1,128)} %copy-done.1, f32[261]{0:T(512)S(1)} %copy-done.43, f32[10368]{0:T(1024)S(1)} %broadcast_multiply_fusion.1, f32[10368,261]{0,1:T(8,128)} %fusion.95, bf16[2,512,261]{2,1,0:T(8,128)(2,1)S(1)} %copy-done.14, ...), kind=kOutput, calls=%fused_computation.20 | convolution fusion | flops 2789820928 | bytes 54188032 | tf_op jit(solution)/shard_map/lp,lc->pc/dot_general | solution.py:54
  686.6 9.9 fusion.96
  696.5 29.1 %multiply_reduce_fusion.1 = (f32[261]{0:T(512)S(1)}, f32[10368]{0:T(1024)S(1)}, f32[10368]{0:T(1024)S(1)}, f32[10368,261]{0,1:T(8,128)}) fusion(f32[10368,261]{0,1:T(8,128)} %get-tuple-element.114, f32[1,1,10368,261]{2,1,3,0:T(1,128)} %copy-done.1, f32[10368]{0:T(1024)S(1)} %fusion.76, f32[10368]{0:T(1024)S(1)} %broadcast_multiply_fusion.1, ...), kind=kOutput, calls=%fused_computation.15 | convolution fusion | flops 2816870912 | bytes 76014096 | tf_op jit(solution)/shard_map/lp,lc->pc/dot_general | solution.py:54
  725.7 22.0 %multiply_reduce_fusion = (f32[261]{0:T(512)S(1)}, f32[10368]{0:T(1024)S(1)}, f32[1,10368,261]{1,2,0:T(8,128)}) fusion(f32[10368,261]{0,1:T(8,128)} %get-tuple-element.115, f32[1,1,10368,261]{2,1,3,0:T(1,128)} %get-tuple-element.85, f32[10368]{0:T(1024)S(1)} %copy-done.30, f32[10368]{0:T(1024)S(1)} %broadcast_multiply_fusion, ...), kind=kLoop, calls=%fused_computation.14 | loop fusion | flops 45992188 | bytes 54454824 | tf_op jit(solution)/shard_map/reduce_sum | solution.py:166
  747.7 10.8 %add_bitcast_fusion = f32[1,10368,261]{1,2,0:T(8,128)} fusion(f32[10368]{0:T(1024)S(1)} %negate_multiply_fusion.1, f32[10368]{0:T(1024)S(1)} %multiply_multiply_fusion.5, f32[10368]{0:T(1024)S(1)} %broadcast_multiply_fusion, f32[1,1,10368,261]{2,1,3,0:T(1,128)} %get-tuple-element.85, f32[10368]{0:T(1024)S(1)} %copy-done.30, f32[10368,261]{0,1:T(8,128)S(1)} %copy-done.3, ...), kind=kLoop, calls=%fused_computation.16 | loop fusion | flops 18942336 | bytes 32639508 | tf_op jit(solution)/shard_map/stack | solution.py:167
  758.5 8.5 maximum_bitcast_fusion
  767.1 26.8 %copy.83 = f32[2,1,10368,261]{2,1,3,0:T(1,128)} copy(f32[2,1,10368,261]{2,3,0,1:T(8,128)S(1)} %maximum_bitcast_fusion) | data formatting | bytes 43296768
  793.8 44.9 %all-reduce.1 = (f32[261]{0:T(512)S(1)}, f32[1,1024]{1,0:T(1,128)S(1)}) all-reduce(f32[261]{0:T(512)S(1)} %add.212, f32[1,1024]{1,0:T(1,128)S(1)} %bitcast.294), channel_id=1, replica_groups=mesh['img'=4,'pix'=8] {'img','pix'}, use_global_device_ids=true, to_apply=%region_32.33 | all-reduce | flops 1285 | bytes 10280 | tf_op jit(solution)/shard_map/psum | solution.py:171
  862.3 152.8 %reduce-scatter.5.cloned.1.call-done = f32[8,128,128]{2,1,0:T(8,128)} async-done(((f32[256,128,128]{2,1,0:T(8,128)}), f32[8,128,128]{2,1,0:T(8,128)}) %reduce-scatter.5.cloned.1.call-update) | async-done | bytes 524304 | tf_op jit(solution)/shard_map/reduce_scatter | solution.py:197
  (261 shorter events, 127.2 us)
Async XLA Ops:
  7.2 1009.7 %copy-start = (f32[8,128,128]{2,1,0:T(8,128)S(1)}, f32[8,128,128]{2,1,0:T(8,128)}, u32[]{:S(2)}) copy-start(f32[8,128,128]{2,1,0:T(8,128)} %param.20) | copy-start | bytes 1572868
  7.2 14.9 %copy-start.45 = (f32[2,1024]{1,0:T(2,128)S(1)}, f32[2,1024]{1,0:T(2,128)}, u32[]{:S(2)}) copy-start(f32[2,1024]{1,0:T(2,128)} %param.24) | copy-start | bytes 24580
  7.2 84.2 %all-gather.3.cloned.1.call-start = ((), (), s32[]{:S(2)}) async-start(), calls=%async_computation.2 | async-start | bytes 8650752 | tf_op jit(solution)/shard_map/all_gather | solution.py:112
  9.1 220.9 %reduce-scatter.7.cloned.1.call-start = ((), (), s32[]{:S(2)}) async-start(), calls=%async_computation.4 | async-start | bytes 294912
  20.1 101.8 %copy-start.49 = (f32[512]{0:T(512)}, f32[512]{0:T(512)S(1)}, u32[]{:S(2)}) copy-start(f32[512]{0:T(512)S(1)} %broadcast_multiply_fusion.2) | copy-start | bytes 6148
  22.0 26.3 %copy-start.51 = (f32[512]{0:T(512)}, f32[512]{0:T(512)S(1)}, u32[]{:S(2)}) copy-start(f32[512]{0:T(512)S(1)} %multiply_reduce_fusion.10) | copy-start | bytes 6148
  22.1 99.8 %copy-start.62 = (f32[512]{0:T(512)}, f32[512]{0:T(512)S(1)}, u32[]{:S(2)}) copy-start(f32[512]{0:T(512)S(1)} %fusion.79) | copy-start | bytes 6148
  22.7 99.2 %copy-start.54 = (f32[1,1024]{1,0:T(1,128)}, f32[1,1024]{1,0:T(1,128)S(1)}, u32[]{:S(2)}) copy-start(f32[1,1024]{1,0:T(1,128)S(1)} %get-tuple-element.95) | copy-start | bytes 12292
  48.3 13.1 %copy-start.1 = (f32[1,1,10368,261]{2,1,3,0:T(1,128)}, f32[1,1,10368,261]{2,1,3,0:T(1,128)S(1)}, u32[]{:S(2)}) copy-start(f32[1,1,10368,261]{2,1,3,0:T(1,128)S(1)} %get-tuple-element.84) | copy-start | bytes 32472580
  48.4 13.6 %copy-start.2 = (f32[1,1,10368,261]{2,1,3,0:T(1,128)S(1)}, f32[1,1,10368,261]{2,1,3,0:T(1,128)}, u32[]{:S(2)}) copy-start(f32[1,1,10368,261]{2,1,3,0:T(1,128)} %get-tuple-element.85) | copy-start | bytes 32472580
  48.4 13.6 %copy-start.43 = (f32[261]{0:T(512)S(1)}, f32[261]{0:T(512)}, u32[]{:S(2)}) copy-start(f32[261]{0:T(512)} %param.23) | copy-start | bytes 3136
  125.6 21.6 %slice-start.2 = ((s8[5474304]{0:T(1024)(128)(4,1)}), s8[4194304]{0:T(1024)(128)(4,1)S(1)}, s32[]{:S(2)}) async-start(s8[5474304]{0:T(1024)(128)(4,1)} %bitcast.276), calls=%async_computation.9 | async-start | bytes 8388608
  137.3 9.8 slice-start.3
  158.7 16.1 %copy-start.66 = (u32[32]{0:T(128)S(1)}, u32[32]{0:T(128)}, u32[]{:S(2)}) copy-start(u32[32]{0:T(128)} %constant.175) | copy-start | bytes 388
  169.2 152.8 %all-reduce.6.cloned.1.call-start = ((), (), s32[]{:S(2)}) async-start(), calls=%async_computation.5 | async-start | bytes 3145728
  174.7 411.6 %all-reduce.8.cloned.1.call-start = ((), (), s32[]{:S(2)}) async-start(), calls=%async_computation.6 | async-start | bytes 7438336 | tf_op jit(solution)/shard_map/psum | solution.py:171
  230.9 92.2 %copy-start.57 = (f32[2,64]{1,0:T(2,128)}, f32[2,64]{1,0:T(2,128)S(1)}, u32[]{:S(2)}) copy-start(f32[2,64]{1,0:T(2,128)S(1)} %copy.94) | copy-start | bytes 1540
  324.7 11.5 %copy-start.25 = (f32[2,64,1024]{2,1,0:T(8,128)}, f32[2,64,1024]{2,1,0:T(8,128)S(1)}, u32[]{:S(2)}) copy-start(f32[2,64,1024]{2,1,0:T(8,128)S(1)} %fusion.61) | copy-start | bytes 1572868
  327.1 123.0 %copy-start.12 = (f32[2,64,1024]{2,1,0:T(8,128)}, f32[2,64,1024]{2,1,0:T(8,128)S(1)}, u32[]{:S(2)}) copy-start(f32[2,64,1024]{2,1,0:T(8,128)S(1)} %get-tuple-element.108) | copy-start | bytes 1572868
  447.4 567.7 %reduce-scatter.5.cloned.1.call-start = ((), (), s32[]{:S(2)}) async-start(), calls=%async_computation.3 | async-start | bytes 17301504 | tf_op jit(solution)/shard_map/reduce_scatter | solution.py:197
  655.9 9.9 copy-start.14
  665.8 20.8 %copy-start.42 = (f32[10368]{0:T(1024)S(1)}, f32[10368]{0:T(1024)}, u32[]{:S(2)}) copy-start(f32[10368]{0:T(1024)} %copy-done.41) | copy-start | bytes 124420
  696.5 29.2 %copy-start.40 = (f32[10368]{0:T(1024)S(1)}, f32[10368]{0:T(1024)}, u32[]{:S(2)}) copy-start(f32[10368]{0:T(1024)} %copy-done.39) | copy-start | bytes 124420
  696.5 29.2 %copy-start.30 = (f32[10368]{0:T(1024)S(1)}, f32[10368]{0:T(1024)}, u32[]{:S(2)}) copy-start(f32[10368]{0:T(1024)} %copy-done.29) | copy-start | bytes 124420
  725.7 22.0 %copy-start.3 = (f32[10368,261]{0,1:T(8,128)S(1)}, f32[10368,261]{0,1:T(8,128)}, u32[]{:S(2)}) copy-start(f32[10368,261]{0,1:T(8,128)} %get-tuple-element.115) | copy-start | bytes 32472580
  767.0 26.8 %copy-start.53 = (f32[1024]{0:T(1024)S(1)}, f32[1024]{0:T(1024)}, u32[]{:S(2)}) copy-start(f32[1024]{0:T(1024)} %get-tuple-element.64) | copy-start | bytes 12292
  767.0 73.7 %copy-start.13 = (f32[2,64,1024]{2,1,0:T(8,128)S(1)}, f32[2,64,1024]{2,1,0:T(8,128)}, u32[]{:S(2)}) copy-start(f32[2,64,1024]{2,1,0:T(8,128)} %copy-done.12) | copy-start | bytes 1572868
  767.0 73.7 %copy-start.19 = (bf16[1024,1024,1]{1,0,2:T(8,128)(2,1)S(1)}, bf16[1024,1024,1]{1,0,2:T(8,128)(2,1)}, u32[]{:S(2)}) copy-start(bf16[1024,1024,1]{1,0,2:T(8,128)(2,1)} %reshape.280) | copy-start | bytes 6291460
  767.0 73.7 %copy-start.70 = (u8[64,1024]{1,0:T(8,128)(4,1)S(1)}, u8[64,1024]{1,0:T(8,128)(4,1)}, u32[]{:S(2)}) copy-start(u8[64,1024]{1,0:T(8,128)(4,1)} %copy-done.69) | copy-start | bytes 196612
  767.1 73.7 %copy-start.72 = (u8[64,1024]{1,0:T(8,128)(4,1)S(1)}, u8[64,1024]{1,0:T(8,128)(4,1)}, u32[]{:S(2)}) copy-start(u8[64,1024]{1,0:T(8,128)(4,1)} %copy-done.71) | copy-start | bytes 196612
  855.2 162.5 %copy-start.24 = (f32[8,128,128]{2,1,0:T(8,128)S(1)}, f32[8,128,128]{2,1,0:T(8,128)}, u32[]{:S(2)}) copy-start(f32[8,128,128]{2,1,0:T(8,128)} %param.16) | copy-start | bytes 1572868
  858.3 167.0 %copy-start.47 = (f32[2,1024]{1,0:T(2,128)}, f32[2,1024]{1,0:T(2,128)S(1)}, u32[]{:S(2)}) copy-start(f32[2,1024]{1,0:T(2,128)S(1)} %get-tuple-element.75) | copy-start | bytes 24580
  (50 other events, 225.7 us)
Sparse Core Ops, SparseCore 0:
  11.6 79.8 all-gather.2
  169.3 60.6 reduce-scatter.6
  233.6 88.3 all-reduce.5
  447.5 138.7 all-reduce.7
  656.0 359.0 reduce-scatter.4
